TPU v7x, 32 devices: a whole 2x2x4 slice. The times are simulated.
32 devices in a mesh: row: 4 (over z), col: 4 (over x, core), depth: 2 (over y).
Axes of the slice: x: 2, y: 2, z: 4, core: 2. Of those that a mesh axis runs over, the one named last changes fastest.
Arguments:
- amplitudes: float32 [14400, 4, 1200], P('row', 'depth', 'col'), may hold values from -6 to 6
- integrals: float32 [4, 1200, 4, 1200], P('depth', 'row', 'col'), may hold values from -0.375 to 0.375
- occ_energy: float32 [120], replicated, may hold values from -2 to -0.5
- vir_energy: float32 [1200], replicated, may hold values from 0.3 to 3
Outputs:
- update: float32 [14400, 4, 1200], P(('row', 'col'), 'depth')
All inputs are finite; a program needn't handle non-finite values.
Results may differ from a plain program's by a relative error of at most 0.00007.
Values sent between devices are 32-bit elements; how exact they have to be, the bound alone decides.
A program may use at most 192 MiB of HBM per device.

v0:
```python
import jax
import jax.numpy as jnp
from jax import lax
from jax.sharding import PartitionSpec as P


def body(amplitudes, integrals, occ_energy, vir_energy):
    pair_rows = amplitudes.shape[0]
    wide_amplitude = lax.all_gather(amplitudes, "col", axis=2, tiled=True)
    panel_count = integrals.shape[0]
    a_count = integrals.shape[2]
    b_count = integrals.shape[3]
    own_rows = integrals.reshape(panel_count, integrals.shape[1], a_count * b_count)
    partial_value = jnp.einsum(
        "ipd,pdn->in",
        wide_amplitude,
        lax.all_gather(own_rows, "row", axis=1, tiled=True),
        precision=lax.Precision.HIGHEST,
        preferred_element_type=jnp.float32,
    )
    partial_value = partial_value.reshape(pair_rows, a_count, b_count)
    summed = lax.psum_scatter(partial_value, "depth", scatter_dimension=2, tiled=True)
    summed = lax.all_to_all(
        lax.all_to_all(summed, "col", split_axis=0, concat_axis=1, tiled=True),
        "depth",
        split_axis=1,
        concat_axis=2,
        tiled=True,
    )
    local_pairs = summed.shape[0]
    local_a = summed.shape[1]
    occ_count = occ_energy.shape[0]
    first_pair = (
        lax.axis_index("row") * lax.axis_size("col") + lax.axis_index("col")
    ) * local_pairs
    pair_index = first_pair + jnp.arange(local_pairs, dtype=jnp.int32)
    first_index = pair_index // occ_count
    second_index = pair_index % occ_count
    occ_ids = jnp.arange(occ_count, dtype=jnp.int32)
    first_energy = jnp.sum(
        jnp.where(first_index[:, None] == occ_ids[None, :], occ_energy[None, :], 0.0), axis=1
    )
    second_energy = jnp.sum(
        jnp.where(second_index[:, None] == occ_ids[None, :], occ_energy[None, :], 0.0), axis=1
    )
    a_start = lax.axis_index("depth") * local_a
    batch_energy = lax.dynamic_slice_in_dim(vir_energy, a_start, local_a)
    pair_energy = first_energy + second_energy
    denominator = (
        pair_energy[:, None, None] - batch_energy[None, :, None] - vir_energy[None, None, :]
    )
    return summed / denominator


def solution(mesh):
    in_specs = (P("row", "depth", "col"), P("depth", "row", "col", None), P(), P())
    out_specs = P(("row", "col"), "depth", None)
    return jax.shard_map(body, mesh=mesh, in_specs=in_specs, out_specs=out_specs, check_vma=False)
```

profile of v0, /device:TPU:0, one launch (start us, length us, event | category | flops | bytes accessed | tf_op | source)
XLA Modules:
  0.0 1191.5 jit_solution(17222983624142915853)
XLA Ops:
  6.5 5.1 copy.22
  11.7 0.7 all-gather.4.cloned.1.call-update
  12.4 215.5 %all-gather.6.cloned.1.call-done = f32[2,1200,1,1200]{3,0,2,1:T(2,128)} async-done(((f32[2,300,1,1200]{3,0,2,1:T(2,128)}), f32[2,1200,1,1200]{3,0,2,1:T(2,128)}) %all-gather.6.cloned.1.call-update) | async-done | bytes 11520016 | tf_op jit(solution)/shard_map/all_gather | solution.py:17
  227.9 20.9 %copy.23 = f32[2,1200,1,1200]{1,3,0,2:T(8,128)} copy(f32[2,1200,1,1200]{3,0,2,1:T(2,128)} %all-gather.6.cloned.1.call-done) | data formatting | bytes 23040000 | tf_op jit(solution)/shard_map/all_gather | solution.py:17
  248.8 194.4 %all-gather.4.cloned.1.call-done = f32[3600,2,1200]{0,1,2:T(2,128)} async-done(((f32[3600,2,300]{0,1,2:T(2,128)}), f32[3600,2,1200]{0,1,2:T(2,128)}) %all-gather.4.cloned.1.call-update) | async-done | bytes 34560016 | tf_op jit(solution)/shard_map/all_gather | solution.py:9
  443.2 169.6 %fusion.3 = f32[3600,1,1200]{0,2,1:T(8,128)} fusion(f32[3600,2,1200]{0,1,2:T(2,128)} %all-gather.4.cloned.1.call-done, f32[2,1200,1,1200]{1,3,0,2:T(8,128)} %copy.23), kind=kOutput, calls=%fused_computation.2 | convolution fusion | flops 124416000000 | bytes 63360000 | tf_op jit(solution)/shard_map/ipd,pdn->in/dot_general | solution.py:14
  612.8 208.9 %fusion = f32[3600,608]{0,1:T(8,128)} fusion(f32[3600,1,1200]{0,2,1:T(8,128)} %fusion.3), kind=kCustom, calls=%all-reduce-scatter | all-reduce-scatter fusion | flops 4377601 | bytes 26035712
  821.7 0.9 slice
  822.6 2.6 collective-permute-start
  825.2 0.6 dynamic-slice.4
  826.5 1.0 collective-permute-done
  827.4 22.9 %concatenate = f32[3600,616]{0,1:T(8,128)} concatenate(f32[3600,8]{0,1:T(8,128)S(1)} %collective-permute-done, f32[3600,608]{0,1:T(8,128)} %fusion), dimensions={1} | concatenate | bytes 17740800
  850.4 7.5 dynamic-slice_bitcast_fusion
  857.9 19.8 %copy.25 = f32[3600,1,600]{2,1,0:T(1,128)} copy(f32[3600,1,600]{0,2,1:T(8,128)} %dynamic-slice_bitcast_fusion) | data formatting | bytes 17280000 | tf_op jit(solution)/shard_map/reduce_scatter | solution.py:22
  877.7 109.9 %all_to_all.36 = f32[3600,1,600]{2,1,0:T(1,128)} all-to-all(f32[3600,1,600]{2,1,0:T(1,128)} %copy.25), channel_id=1, replica_groups=mesh['row'=4,'col'=4,'depth'=2] {'col'}, dimensions={0} | all-to-all | bytes 17280000 | tf_op jit(solution)/shard_map/all_to_all | solution.py:24
  987.5 28.3 %reduce = f32[3600,600]{1,0:T(8,128)} reduce(f32[3600,1,600]{2,1,0:T(1,128)} %all_to_all.36, f32[]{:T(128)} %constant.47), dimensions={1}, to_apply=%all_to_all.26.reduce_sub_computation | reduce | bytes 17280004 | tf_op jit(solution)/shard_map/all_to_all | solution.py:24
  1015.8 9.8 all_to_all.27
  1025.7 7.4 all-to-all-start.1
  1033.1 0.6 select_reduce_fusion
  1033.8 101.9 %all-to-all-done.1 = f32[900,4,600]{2,0,1:T(8,128)} async-done(((f32[900,4,600]{2,0,1:T(8,128)}), f32[900,4,600]{2,0,1:T(8,128)}, u32[]{:S(2)}, u32[]{:S(2)}) %all-to-all-start.1) | async-done | bytes 8640032 | tf_op jit(solution)/shard_map/all_to_all | solution.py:23
  1135.8 19.9 %copy.26 = f32[900,2,2,600]{3,2,0,1:T(2,128)} copy(f32[900,2,2,600]{3,0,1,2:T(8,128)} %bitcast.6) | data formatting | bytes 17280000 | tf_op jit(solution)/shard_map/all_to_all | solution.py:23
  1155.6 15.3 %all_to_all.33 = f32[900,2,1200]{2,0,1:T(8,128)} reshape(f32[900,2,2,600]{3,2,0,1:T(2,128)} %copy.26) | data formatting | bytes 17280000 | tf_op jit(solution)/shard_map/all_to_all | solution.py:23
  1170.9 4.9 subtract_divide_fusion
  1175.8 8.8 copy.27
  (13 shorter events, 0.2 us)
Async XLA Ops:
  6.5 221.4 %all-gather.6.cloned.1.call-start = ((), (), s32[]{:S(2)}) async-start(), calls=%async_computation.3 | async-start | bytes 15360000 | tf_op jit(solution)/shard_map/all_gather | solution.py:17
  11.6 431.5 %all-gather.4.cloned.1.call-start = ((), (), s32[]{:S(2)}) async-start(), calls=%async_computation.2 | async-start | bytes 44544000 | tf_op jit(solution)/shard_map/all_gather | solution.py:9
  612.8 212.5 %copy-start.2 = (u32[32]{0:T(128)S(1)}, u32[32]{0:T(128)}, u32[]{:S(2)}) copy-start(u32[32]{0:T(128)} %constant.45) | copy-start | bytes 388
  822.6 4.8 collective-permute-start
  1025.7 7.4 copy-start.1
  1025.7 8.0 copy-start
  1025.7 110.1 %all-to-all-start.1 = ((f32[900,4,600]{2,0,1:T(8,128)}), f32[900,4,600]{2,0,1:T(8,128)}, u32[]{:S(2)}, u32[]{:S(2)}) async-start(f32[900,4,600]{2,0,1:T(8,128)} %bitcast.24), calls=%async_computation.1 | async-start | bytes 18513920 | tf_op jit(solution)/shard_map/all_to_all | solution.py:23
Sparse Core Ops, SparseCore 0:
  11.8 216.0 all-gather.5
  229.5 213.6 all-gather.3
where the time goes:
time: 1190 us
  waiting for transfers between devices  513 us (43%)
  blocking collectives  319 us (27%)
  matrix products  170 us (14%)
  local copies, waits for them, and re-layouts  132 us (11%)
  other arithmetic  33.9 us (3%)
  between operations  14.1 us (1%)
    all_gather x1, waiting for transfers between devices, body(): lax.all_gather(own_rows, 'row', axis=1, tiled=True)  215 us
    unnamed x1, blocking collectives  209 us
    all_gather x1, waiting for transfers between devices, body(): wide_amplitude = lax.all_gather(amplitudes, 'col', axis=2, tiled=True)  194 us
    dot_general x1, matrix products, body(): jnp.einsum('ipd,pdn->in', wide_amplitude, lax.all_gather(own_rows, 'row',...  170 us
    all_to_all x1, blocking collectives, body(): lax.all_to_all(summed, 'col', split_axis=0, concat_axis=1, tiled=True)  110 us
    all_to_all x1, waiting for transfers between devices, body(): lax.all_to_all(lax.all_to_all(summed, 'col', split_axis=0, concat_axis=1,...  102 us
    unnamed x11, local copies, waits for them, and re-layouts  37.1 us
    all_to_all x2, local copies, waits for them, and re-layouts, body(): lax.all_to_all(lax.all_to_all(summed, 'col', split_axis=0, concat_axis=1,...  35.2 us
  transfers between devices with their start and end apart: 4, of which 4 were waited for; matrix products, arithmetic and copies ran while one was open for 2% of the time, Pallas kernels for 0%

commit v1 on v0

--- a/solution.py
+++ b/solution.py
@@ -11,13 +11,42 @@
     a_count = integrals.shape[2]
     b_count = integrals.shape[3]
     own_rows = integrals.reshape(panel_count, integrals.shape[1], a_count * b_count)
+    latest, v_now, y = (jax.lax.axis_size("row"), jax.lax.axis_index("row"), own_rows.shape[1])
+    store = tuple(((pp, (pp + 1) % latest) for pp in range(latest)))
+    by_place = tuple(((pp, (pp - 1) % latest) for pp in range(latest)))
+    big = mat_out = own_rows
     partial_value = jnp.einsum(
         "ipd,pdn->in",
-        wide_amplitude,
-        lax.all_gather(own_rows, "row", axis=1, tiled=True),
+        lax.dynamic_slice_in_dim(wide_amplitude, v_now * y, own_rows.shape[1], axis=2),
+        own_rows,
         precision=lax.Precision.HIGHEST,
         preferred_element_type=jnp.float32,
     )
+    shaped = latest // 2
+    u = 1
+    while u < shaped + 1:
+        big = jax.lax.ppermute(big, "row", store)
+        if u < latest - shaped:
+            mat_out = jax.lax.ppermute(mat_out, "row", by_place)
+            partial_value = partial_value + jnp.einsum(
+                "ipd,pdn->in",
+                lax.dynamic_slice_in_dim(
+                    wide_amplitude, (v_now + u) % latest * y, mat_out.shape[1], axis=2
+                ),
+                mat_out,
+                precision=lax.Precision.HIGHEST,
+                preferred_element_type=jnp.float32,
+            )
+        partial_value = partial_value + jnp.einsum(
+            "ipd,pdn->in",
+            lax.dynamic_slice_in_dim(
+                wide_amplitude, (v_now - u) % latest * y, big.shape[1], axis=2
+            ),
+            big,
+            precision=lax.Precision.HIGHEST,
+            preferred_element_type=jnp.float32,
+        )
+        u += 1
     partial_value = partial_value.reshape(pair_rows, a_count, b_count)
     summed = lax.psum_scatter(partial_value, "depth", scatter_dimension=2, tiled=True)
     summed = lax.all_to_all(

time: 1190 us -> 1050 us (0.88)
  waiting for transfers between devices: 513 us -> 313 us
  matrix products: 170 us -> 207 us
    all_gather x1 -> x0, waiting for transfers between devices: 215 us -> none  [body(): lax.all_gather(own_rows, 'row', axis=1, tiled=True)]
    ppermute x0 -> x3, waiting for transfers between devices: none -> 67.7 us  [the longest x2 67.7 us: body(): big = jax.lax.ppermute(big, 'row', store)]
    all_gather x1, waiting for transfers between devices: 194 us -> 142 us  [body(): wide_amplitude = lax.all_gather(amplitudes, 'col', axis=2, tiled=True)]
    dot_general x1 -> x4, matrix products: 170 us -> 207 us  [the longest x3 156 us: body(): jnp.einsum('ipd,pdn->in', lax.dynamic_slice_in_dim(wide_amplitude, (v_now...]
    dynamic_slice x0 -> x1, local copies, waits for them, and re-layouts: none -> 30.6 us  [body(): lax.dynamic_slice_in_dim(wide_amplitude, (v_now - u) % latest * y, big.sh...]
    all_gather x1 -> x0, local copies, waits for them, and re-layouts: 20.9 us -> none  [body(): lax.all_gather(own_rows, 'row', axis=1, tiled=True)]
    unnamed x11 -> x25, local copies, waits for them, and re-layouts: 37.1 us -> 33.4 us
  transfers between devices with their start and end apart: 4 -> 6, of which waited for: 4 -> 4; matrix products, arithmetic and copies ran while one was open for 2% -> 18% of each run, Pallas kernels for 0% -> 0%
where the time goes in v1:
time: 1050 us; the launch traced here: 1040 us
  blocking collectives  319 us (30%)
  waiting for transfers between devices  313 us (30%)
  matrix products  207 us (20%)
  local copies, waits for them, and re-layouts  142 us (14%)
  other arithmetic  33.9 us (3%)
  starting transfers between devices  14.9 us (1%)
  between operations  14.4 us (1%)
    unnamed x1, blocking collectives  209 us
    dot_general x3, matrix products, body(): jnp.einsum('ipd,pdn->in', lax.dynamic_slice_in_dim(wide_amplitude, (v_now...  156 us
    all_gather x1, waiting for transfers between devices, body(): wide_amplitude = lax.all_gather(amplitudes, 'col', axis=2, tiled=True)  142 us
    all_to_all x1, blocking collectives, body(): lax.all_to_all(summed, 'col', split_axis=0, concat_axis=1, tiled=True)  110 us
    all_to_all x1, waiting for transfers between devices, body(): lax.all_to_all(lax.all_to_all(summed, 'col', split_axis=0, concat_axis=1,...  102 us
    ppermute x2, waiting for transfers between devices, body(): big = jax.lax.ppermute(big, 'row', store)  67.7 us
    dot_general x1, matrix products, body(): jnp.einsum('ipd,pdn->in', lax.dynamic_slice_in_dim(wide_amplitude, v_now...  50.4 us
    all_to_all x2, local copies, waits for them, and re-layouts, body(): lax.all_to_all(lax.all_to_all(summed, 'col', split_axis=0, concat_axis=1,...  35.2 us
  transfers between devices with their start and end apart: 6, of which 4 were waited for; matrix products, arithmetic and copies ran while one was open for 18% of the time, Pallas kernels for 0%

profile of v1, /device:TPU:0, one launch (start us, length us, event | category | flops | bytes accessed | tf_op | source)
XLA Modules:
  0.0 1043.6 jit_solution(12742498446848905641)
XLA Ops:
  8.6 4.0 copy.27
  12.6 3.1 collective-permute-start.1
  15.7 2.0 collective-permute-start
  17.7 67.7 %collective-permute-done.1 = f32[2,300,1200]{2,0,1:T(2,128)} collective-permute-done((f32[2,300,1200]{2,0,1:T(2,128)}, f32[2,300,1200]{2,0,1:T(2,128)}, u32[]{:S(2)}, u32[]{:S(2)}) %collective-permute-start.1) | collective-permute-done | bytes 2880032 | tf_op jit(solution)/shard_map/ppermute | solution.py:28
  85.4 141.7 %all-gather.2.cloned.1.call-done = f32[3600,2,1200]{0,1,2:T(2,128)} async-done(((f32[3600,2,300]{0,1,2:T(2,128)}), f32[3600,2,1200]{0,1,2:T(2,128)}) %all-gather.2.cloned.1.call-update) | async-done | bytes 34560016 | tf_op jit(solution)/shard_map/all_gather | solution.py:9
  227.2 30.6 %constant_dynamic-slice_fusion = (f32[3600,2,300]{0,1,2:T(2,128)}, f32[3600,2,300]{0,1,2:T(2,128)}, f32[3600,2,300]{0,1,2:T(2,128)}, f32[3600,2,300]{0,1,2:T(2,128)}) fusion(f32[3600,2,1200]{0,1,2:T(2,128)} %all-gather.2.cloned.1.call-done, s32[]{:T(128)S(6)} %select_n.62, s32[]{:T(128)S(6)} %select_n.60, s32[]{:T(128)S(6)} %select_n.58, s32[]{:T(128)S(6)} %select_n.56), kind=kLoop, calls=%fused_computation.31 | loop fusion | bytes 69120016 | tf_op jit(solution)/shard_map/dynamic_slice | solution.py:42
  257.8 50.4 %fusion.7 = f32[3600,1200,1]{0,1,2:T(8,128)} fusion(f32[3600,2,300]{0,1,2:T(2,128)} %get-tuple-element.10, f32[2,300,1,1200]{3,2,1,0:T(1,128)} %param.5), kind=kOutput, calls=%fused_computation.10 | convolution fusion | flops 31104000000 | bytes 28800000 | tf_op jit(solution)/shard_map/ipd,pdn->in/dot_general | solution.py:18
  308.2 51.2 %fusion.3 = f32[3600,1200,1]{0,1,2:T(8,128)} fusion(f32[3600,2,300]{0,1,2:T(2,128)} %get-tuple-element.8, f32[2,300,1200]{2,0,1:T(2,128)} %collective-permute-done.1), kind=kOutput, calls=%fused_computation.6 | convolution fusion | flops 31104000000 | bytes 28800000 | tf_op jit(solution)/shard_map/ipd,pdn->in/dot_general | solution.py:40
  359.5 49.6 %fusion.5 = f32[3600,1200,1]{0,1,2:T(8,128)} fusion(f32[3600,2,300]{0,1,2:T(2,128)S(1)} %bitcast.43, f32[2,300,1200]{2,0,1:T(2,128)} %collective-permute-done), kind=kOutput, calls=%fused_computation.8 | convolution fusion | flops 31104000000 | bytes 28800000 | tf_op jit(solution)/shard_map/ipd,pdn->in/dot_general | solution.py:31
  409.1 55.4 %fusion.1 = f32[3600,1,1200]{0,2,1:T(8,128)} fusion(f32[3600,1200,1]{0,1,2:T(8,128)} %fusion.3, f32[3600,1200,1]{0,1,2:T(8,128)} %fusion.5, f32[3600,1200,1]{0,1,2:T(8,128)} %fusion.7, f32[3600,2,300]{0,1,2:T(2,128)S(1)} %bitcast.39, f32[2,300,1200]{2,0,1:T(2,128)S(1)} %collective-permute-done.2), kind=kOutput, calls=%fused_computation.1 | convolution fusion | flops 31116959744 | bytes 80640000 | tf_op jit(solution)/shard_map/ipd,pdn->in/dot_general | solution.py:40
  464.5 209.0 %fusion = f32[3600,608]{0,1:T(8,128)} fusion(f32[3600,1,1200]{0,2,1:T(8,128)} %fusion.1), kind=kCustom, calls=%all-reduce-scatter | all-reduce-scatter fusion | flops 4377601 | bytes 26035712
  674.4 2.4 collective-permute-start.3
  679.2 22.9 %concatenate = f32[3600,616]{0,1:T(8,128)} concatenate(f32[3600,8]{0,1:T(8,128)S(1)} %collective-permute-done.3, f32[3600,608]{0,1:T(8,128)} %fusion), dimensions={1} | concatenate | bytes 17740800
  702.1 7.6 dynamic-slice_bitcast_fusion
  709.7 19.8 %copy.34 = f32[3600,1,600]{2,1,0:T(1,128)} copy(f32[3600,1,600]{0,2,1:T(8,128)} %dynamic-slice_bitcast_fusion) | data formatting | bytes 17280000 | tf_op jit(solution)/shard_map/reduce_scatter | solution.py:51
  729.5 110.0 %all_to_all.36 = f32[3600,1,600]{2,1,0:T(1,128)} all-to-all(f32[3600,1,600]{2,1,0:T(1,128)} %copy.34), channel_id=1, replica_groups=mesh['row'=4,'col'=4,'depth'=2] {'col'}, dimensions={0} | all-to-all | bytes 17280000 | tf_op jit(solution)/shard_map/all_to_all | solution.py:53
  839.5 28.3 %reduce = f32[3600,600]{1,0:T(8,128)} reduce(f32[3600,1,600]{2,1,0:T(1,128)} %all_to_all.36, f32[]{:T(128)} %constant.71), dimensions={1}, to_apply=%all_to_all.26.reduce_sub_computation | reduce | bytes 17280004 | tf_op jit(solution)/shard_map/all_to_all | solution.py:53
  867.8 9.8 all_to_all.27
  877.6 7.4 all-to-all-start.1
  885.8 101.9 %all-to-all-done.1 = f32[900,4,600]{2,0,1:T(8,128)} async-done(((f32[900,4,600]{2,0,1:T(8,128)}), f32[900,4,600]{2,0,1:T(8,128)}, u32[]{:S(2)}, u32[]{:S(2)}) %all-to-all-start.1) | async-done | bytes 8640032 | tf_op jit(solution)/shard_map/all_to_all | solution.py:52
  987.7 19.9 %copy.35 = f32[900,2,2,600]{3,2,0,1:T(2,128)} copy(f32[900,2,2,600]{3,0,1,2:T(8,128)} %bitcast.8) | data formatting | bytes 17280000 | tf_op jit(solution)/shard_map/all_to_all | solution.py:52
  1007.6 15.3 %all_to_all.33 = f32[900,2,1200]{2,0,1:T(8,128)} reshape(f32[900,2,2,600]{3,2,0,1:T(2,128)} %copy.35) | data formatting | bytes 17280000 | tf_op jit(solution)/shard_map/all_to_all | solution.py:52
  1022.9 4.9 subtract_divide_fusion
  1027.8 8.8 copy.36
  (36 shorter events, 5.5 us)
Async XLA Ops:
  6.5 1.9 copy-start
  6.5 220.6 %all-gather.2.cloned.1.call-start = ((), (), s32[]{:S(2)}) async-start(), calls=%async_computation.2 | async-start | bytes 44544000 | tf_op jit(solution)/shard_map/all_gather | solution.py:9
  12.6 72.8 %collective-permute-start.1 = (f32[2,300,1200]{2,0,1:T(2,128)}, f32[2,300,1200]{2,0,1:T(2,128)}, u32[]{:S(2)}, u32[]{:S(2)}) collective-permute-start(f32[2,300,1200]{2,0,1:T(2,128)} %copy.27), channel_id=1, source_target_pairs={{0,8},{8,16},{16,24},{24,0},{1,9},{9,17},{17,25},{25,1},{2,10},{10... | collective-permute-start | bytes 8640008 | tf_op jit(solution)/shard_map/ppermute | solution.py:28
  15.7 343.7 %collective-permute-start = (f32[2,300,1200]{2,0,1:T(2,128)}, f32[2,300,1200]{2,0,1:T(2,128)}, u32[]{:S(2)}, u32[]{:S(2)}) collective-permute-start(f32[2,300,1200]{2,0,1:T(2,128)} %copy.27), channel_id=1, source_target_pairs={{0,24},{8,0},{16,8},{24,16},{1,25},{9,1},{17,9},{25,17},{2,26},{10... | collective-permute-start | bytes 8640008 | tf_op jit(solution)/shard_map/ppermute | solution.py:30
  85.4 323.6 %collective-permute-start.2 = (f32[2,300,1200]{2,0,1:T(2,128)}, f32[2,300,1200]{2,0,1:T(2,128)S(1)}, u32[]{:S(2)}, u32[]{:S(2)}) collective-permute-start(f32[2,300,1200]{2,0,1:T(2,128)} %collective-permute-done.1), channel_id=1, source_target_pairs={{0,8},{8,16},{16,24},{24,0},{1,9},{9,17},{17,25},{25,1},{2,10},{10... | collective-permute-start | bytes 8640008 | tf_op jit(solution)/shard_map/ppermute | solution.py:28
  257.8 101.7 %slice-start.3 = ((s8[8908800]{0:T(1024)(128)(4,1)}), s8[4194304]{0:T(1024)(128)(4,1)S(1)}, s32[]{:S(2)}) async-start(s8[8908800]{0:T(1024)(128)(4,1)} %bitcast.42), calls=%async_computation.6 | async-start | bytes 8388608
  257.8 101.7 %slice-start.4 = ((s8[8908800]{0:T(1024)(128)(4,1)}), s8[4194304]{0:T(1024)(128)(4,1)S(1)}, s32[]{:S(2)}) async-start(s8[8908800]{0:T(1024)(128)(4,1)} %bitcast.42), calls=%async_computation.7 | async-start | bytes 8388608
  308.2 51.2 %slice-start.5 = ((s8[8908800]{0:T(1024)(128)(4,1)}), s8[520192]{0:T(1024)(128)(4,1)S(1)}, s32[]{:S(2)}) async-start(s8[8908800]{0:T(1024)(128)(4,1)} %bitcast.42), calls=%async_computation.8 | async-start | bytes 1040384
  308.2 100.9 %slice-start = ((s8[8908800]{0:T(1024)(128)(4,1)}), s8[4194304]{0:T(1024)(128)(4,1)S(1)}, s32[]{:S(2)}) async-start(s8[8908800]{0:T(1024)(128)(4,1)} %bitcast.38), calls=%async_computation.3 | async-start | bytes 8388608
  308.2 100.9 %slice-start.1 = ((s8[8908800]{0:T(1024)(128)(4,1)}), s8[4194304]{0:T(1024)(128)(4,1)S(1)}, s32[]{:S(2)}) async-start(s8[8908800]{0:T(1024)(128)(4,1)} %bitcast.38), calls=%async_computation.4 | async-start | bytes 8388608
  359.5 49.6 %slice-start.2 = ((s8[8908800]{0:T(1024)(128)(4,1)}), s8[520192]{0:T(1024)(128)(4,1)S(1)}, s32[]{:S(2)}) async-start(s8[8908800]{0:T(1024)(128)(4,1)} %bitcast.38), calls=%async_computation.5 | async-start | bytes 1040384
  464.5 212.3 %copy-start.3 = (u32[32]{0:T(128)S(1)}, u32[32]{0:T(128)}, u32[]{:S(2)}) copy-start(u32[32]{0:T(128)} %constant.69) | copy-start | bytes 388
  674.4 4.8 collective-permute-start.3
  877.6 7.4 copy-start.2
  877.6 8.1 copy-start.1
  877.6 110.1 %all-to-all-start.1 = ((f32[900,4,600]{2,0,1:T(8,128)}), f32[900,4,600]{2,0,1:T(8,128)}, u32[]{:S(2)}, u32[]{:S(2)}) async-start(f32[900,4,600]{2,0,1:T(8,128)} %bitcast.40), calls=%async_computation.1 | async-start | bytes 18513920 | tf_op jit(solution)/shard_map/all_to_all | solution.py:52
Sparse Core Ops, SparseCore 0:
  8.9 218.2 all-gather.1
